TPU v7x, 256 devices: a whole 4x4x8 slice. The times are simulated.
256 devices in a mesh: br: 8 (over y_lo, x), bus: 32 (over y_hi, z, core).
Axes of the slice: x: 4, y: 4 (y_hi: 2, y_lo: 2; y = y_hi * 2 + y_lo), z: 8, core: 2. Of those that a mesh axis runs over, the one named last changes fastest.
Arguments:
- ptdf: bfloat16 [8192, 65536], P('br', 'bus'), may hold values from -0.0234375 to 0.0234375
- load_codes: int32 [65536, 1024], P('bus'), may hold values from -4096 to 4096
- limit_codes: int32 [8192], P('br'), may hold values from 64 to 320
Outputs:
- penalty: float32 [8192, 1024], P(('br', 'bus'))
- sensitivity: float32 [65536, 1024], P('bus', 'br')
All inputs are finite; a program needn't handle non-finite values.
Results may differ from a plain program's by a relative error of at most 0.004.
Values may be sent and summed in bfloat16 or wider, within the bound.
A program may use at most 128 MiB of HBM per device.

v0:
```python
import jax
import jax.numpy as jnp
from jax import lax
from jax.sharding import PartitionSpec as P


def overload(flows, limit_codes):
    limits = (limit_codes.astype(jnp.float32) / 64.0)[:, None]
    magnitude = jnp.sqrt(flows * flows + 1.0)
    zvalue = 4.0 * (magnitude / limits - 1.0)
    penalty = jax.nn.softplus(zvalue) / 4.0
    adjoint = (jax.nn.sigmoid(zvalue) * flows / (magnitude * limits)).astype(jnp.bfloat16)
    return (penalty, adjoint)


def local(ptdf, load_codes, limit_codes):
    injections = (load_codes.astype(jnp.float32) / 1024.0).astype(jnp.bfloat16)
    branch_local = ptdf.shape[0]
    owned = branch_local // lax.axis_size("bus")
    offset = lax.axis_index("bus") * owned
    partial_flows = jnp.dot(ptdf, injections, preferred_element_type=jnp.float32)
    flows = lax.psum_scatter(partial_flows, "bus", scatter_dimension=0, tiled=True)
    limits_own = lax.dynamic_slice_in_dim(limit_codes, offset, owned, 0)
    penalty, adjoint_own = overload(flows, limits_own)
    adjoint_block = lax.all_gather(adjoint_own, "bus", axis=0, tiled=True)
    partial_sens = lax.dot_general(
        ptdf, adjoint_block, (((0,), (0,)), ((), ())), preferred_element_type=jnp.float32
    )
    sensitivity = lax.psum_scatter(partial_sens, "br", scatter_dimension=1, tiled=True)
    return (penalty, sensitivity)


def solution(mesh):
    return jax.shard_map(
        local,
        mesh=mesh,
        in_specs=(P("br", "bus"), P("bus", None), P("br")),
        out_specs=(P(("br", "bus"), None), P("bus", "br")),
        check_vma=False,
    )
```

profile of v0, /device:TPU:1, one launch (start us, length us, event | category | flops | bytes accessed | tf_op | source)
XLA Modules:
  0.0 348.7 jit_solution(4985150040851442825)
XLA Ops:
  7.2 0.0 reduce-scatter.7.cloned.1.call-start
  7.2 11.1 %fusion.2 = f32[1024,1024]{0,1:T(8,128)} fusion(bf16[1024,2048]{1,0:T(8,128)(2,1)} %param.3, s32[2048,1024]{1,0:T(8,128)} %param.4), kind=kOutput, calls=%fused_computation.4 | convolution fusion | flops 4301258752 | bytes 16777216 | tf_op jit(solution)/shard_map/dot_general | solution.py:21
  18.3 5.3 %copy.14 = f32[1024,1024]{1,0:T(8,128)} copy(f32[1024,1024]{0,1:T(8,128)} %fusion.2) | data formatting | bytes 8388608
  23.6 0.0 reduce-scatter.7.cloned.1.call-update
  23.7 0.0 all-gather.2.cloned.1.call-start
  23.7 0.8 convert_multiply_fusion
  24.5 126.7 %reduce-scatter.7.cloned.1.call-done = f32[32,1024]{1,0:T(8,128)} async-done(((f32[1024,1024]{1,0:T(8,128)}), f32[32,1024]{1,0:T(8,128)}) %reduce-scatter.7.cloned.1.call-update) | async-done | bytes 131088 | tf_op jit(solution)/shard_map/reduce_scatter | solution.py:22
  151.1 1.8 divide_convert_fusion
  152.9 0.0 all-gather.2.cloned.1.call-update
  153.0 0.0 reduce-scatter.5.cloned.1.call-start
  153.0 84.4 %all-gather.2.cloned.1.call-done = bf16[1024,1024]{1,0:T(8,128)(2,1)} async-done(((bf16[32,1024]{1,0:T(8,128)(2,1)}), bf16[1024,1024]{1,0:T(8,128)(2,1)}) %all-gather.2.cloned.1.call-update) | async-done | bytes 2097168 | tf_op jit(solution)/shard_map/all_gather | solution.py:25
  237.4 10.6 %convolution_bitcast_fusion = f32[2048,1024]{0,1:T(8,128)} fusion(bf16[1024,1024]{1,0:T(8,128)(2,1)} %all-gather.2.cloned.1.call-done, bf16[1024,2048]{1,0:T(8,128)(2,1)} %param.3), kind=kOutput, calls=%fused_computation.1 | convolution fusion | flops 4294967296 | bytes 14680064 | tf_op jit(solution)/shard_map/dot_general | solution.py:26
  248.0 0.0 reduce-scatter.5.cloned.1.call-update
  248.0 91.6 %reduce-scatter.5.cloned.1.call-done = f32[2048,128]{0,1:T(8,128)} async-done(((f32[2048,1024]{0,1:T(8,128)}), f32[2048,128]{0,1:T(8,128)}) %reduce-scatter.5.cloned.1.call-update) | async-done | bytes 1048592 | tf_op jit(solution)/shard_map/reduce_scatter | solution.py:29
  339.6 2.5 copy.13
Async XLA Ops:
  7.2 144.0 %reduce-scatter.7.cloned.1.call-start = ((), (), s32[]{:S(2)}) async-start(), calls=%async_computation.4 | async-start | bytes 4325376 | tf_op jit(solution)/shard_map/reduce_scatter | solution.py:22
  23.7 213.7 %all-gather.2.cloned.1.call-start = ((), (), s32[]{:S(2)}) async-start(), calls=%async_computation.2 | async-start | bytes 2162688 | tf_op jit(solution)/shard_map/all_gather | solution.py:25
  153.0 186.7 %reduce-scatter.5.cloned.1.call-start = ((), (), s32[]{:S(2)}) async-start(), calls=%async_computation.3 | async-start | bytes 9437184 | tf_op jit(solution)/shard_map/reduce_scatter | solution.py:29
Sparse Core Ops, SparseCore 0:
  23.8 127.3 reduce-scatter.6
  154.9 82.4 all-gather.1
  248.2 91.4 reduce-scatter.4
where the time goes:
time: 349 us
  waiting for transfers between devices  303 us (87%)
  matrix products  21.7 us (6%)
  between operations  13.7 us (4%)
  local copies, waits for them, and re-layouts  7.88 us (2%)
    reduce_scatter x1, waiting for transfers between devices, local(): lax.psum_scatter(partial_flows, 'bus', scatter_dimension=0, tiled=True)  127 us
    reduce_scatter x1, waiting for transfers between devices, local(): lax.psum_scatter(partial_sens, 'br', scatter_dimension=1, tiled=True)  91.6 us
    all_gather x1, waiting for transfers between devices, local(): adjoint_block = lax.all_gather(adjoint_own, 'bus', axis=0, tiled=True)  84.4 us
    dot_general x1, matrix products, local(): jnp.dot(ptdf, injections, preferred_element_type=jnp.float32)  11.1 us
    dot_general x1, matrix products, local(): lax.dot_general(ptdf, adjoint_block, (((0,), (0,)), ((), ())), preferred_...  10.6 us
    unnamed x2, local copies, waits for them, and re-layouts  7.88 us
  transfers between devices with their start and end apart: 3, of which 3 were waited for; matrix products, arithmetic and copies ran while one was open for 0% of the time, Pallas kernels for 0%

commit v1 on v0

--- a/solution.py
+++ b/solution.py
@@ -22,7 +22,10 @@
     flows = lax.psum_scatter(partial_flows, "bus", scatter_dimension=0, tiled=True)
     limits_own = lax.dynamic_slice_in_dim(limit_codes, offset, owned, 0)
     penalty, adjoint_own = overload(flows, limits_own)
-    adjoint_block = lax.all_gather(adjoint_own, "bus", axis=0, tiled=True)
+    item_now = lax.axis_size("bus")
+    reply = jnp.stack(item_now * [adjoint_own], axis=0)
+    out_arr = lax.all_to_all(reply, "bus", 0, 0)
+    adjoint_block = jnp.concatenate(out_arr, axis=0)
     partial_sens = lax.dot_general(
         ptdf, adjoint_block, (((0,), (0,)), ((), ())), preferred_element_type=jnp.float32
     )

time: 349 us -> 324 us (0.928)
  waiting for transfers between devices: 303 us -> 220 us
  blocking collectives: 0 us -> 60.7 us
  matrix products: 21.7 us -> 18 us
    all_gather x1 -> x0, waiting for transfers between devices: 84.4 us -> none  [local(): adjoint_block = lax.all_gather(adjoint_own, 'bus', axis=0, tiled=True)]
    all_to_all x0 -> x1, blocking collectives: none -> 60.7 us  [local(): out_arr = lax.all_to_all(reply, 'bus', 0, 0)]
    dot_general x1, matrix products: 10.6 us -> 6.87 us  [local(): lax.dot_general(ptdf, adjoint_block, (((0,), (0,)), ((), ())), preferred_...]
    unnamed x2 -> x4, local copies, waits for them, and re-layouts: 7.88 us -> 7.87 us
  transfers between devices with their start and end apart: 3 -> 2, of which waited for: 3 -> 2; matrix products, arithmetic and copies ran while one was open for 0% -> 0% of each run, Pallas kernels for 0% -> 0%
where the time goes in v1:
time: 324 us
  waiting for transfers between devices  220 us (68%)
  blocking collectives  60.7 us (19%)
  matrix products  18 us (6%)
  between operations  14.1 us (4%)
  local copies, waits for them, and re-layouts  8.12 us (3%)
    reduce_scatter x1, waiting for transfers between devices, local(): lax.psum_scatter(partial_flows, 'bus', scatter_dimension=0, tiled=True)  127 us
    reduce_scatter x1, waiting for transfers between devices, local(): lax.psum_scatter(partial_sens, 'br', scatter_dimension=1, tiled=True)  93.4 us
    all_to_all x1, blocking collectives, local(): out_arr = lax.all_to_all(reply, 'bus', 0, 0)  60.7 us
    dot_general x1, matrix products, local(): jnp.dot(ptdf, injections, preferred_element_type=jnp.float32)  11.1 us
    unnamed x4, local copies, waits for them, and re-layouts  7.87 us
    dot_general x1, matrix products, local(): lax.dot_general(ptdf, adjoint_block, (((0,), (0,)), ((), ())), preferred_...  6.87 us
  transfers between devices with their start and end apart: 2, of which 2 were waited for; matrix products, arithmetic and copies ran while one was open for 0% of the time, Pallas kernels for 0%

profile of v1, /device:TPU:1, one launch (start us, length us, event | category | flops | bytes accessed | tf_op | source)
XLA Modules:
  0.0 323.7 jit_solution(6220440145703991227)
XLA Ops:
  7.2 0.0 reduce-scatter.7.cloned.1.call-start
  7.2 11.1 %fusion.2 = f32[1024,1024]{0,1:T(8,128)} fusion(bf16[1024,2048]{1,0:T(8,128)(2,1)} %param.3, s32[2048,1024]{1,0:T(8,128)} %param.4), kind=kOutput, calls=%fused_computation.4 | convolution fusion | flops 4301258752 | bytes 16777216 | tf_op jit(solution)/shard_map/dot_general | solution.py:21
  18.3 5.3 %copy.15 = f32[1024,1024]{1,0:T(8,128)} copy(f32[1024,1024]{0,1:T(8,128)} %fusion.2) | data formatting | bytes 8388608
  23.6 0.0 reduce-scatter.7.cloned.1.call-update
  23.7 0.0 reduce-scatter.5.cloned.1.call-start
  23.7 0.8 convert_multiply_fusion
  24.5 126.7 %reduce-scatter.7.cloned.1.call-done = f32[32,1024]{1,0:T(8,128)} async-done(((f32[1024,1024]{1,0:T(8,128)}), f32[32,1024]{1,0:T(8,128)}) %reduce-scatter.7.cloned.1.call-update) | async-done | bytes 131088 | tf_op jit(solution)/shard_map/reduce_scatter | solution.py:22
  151.1 0.0 copy-start
  151.1 1.9 divide_convert_fusion
  153.1 0.2 stack.2
  153.3 60.7 %all_to_all.5 = bf16[32,32,1024]{2,1,0:T(8,128)(2,1)S(1)} all-to-all(bf16[32,32,1024]{2,1,0:T(8,128)(2,1)S(1)} %stack.2), channel_id=1, replica_groups=mesh['br'=8,'bus'=32] {'bus'}, dimensions={0} | all-to-all | bytes 4194304 | tf_op jit(solution)/shard_map/all_to_all | solution.py:27
  214.0 0.0 copy-done
  214.0 6.9 %convolution_bitcast_fusion = f32[2048,1024]{0,1:T(8,128)} fusion(bf16[1024,1024]{1,0:T(8,128)(2,1)S(1)} %bitcast.9, bf16[1024,2048]{1,0:T(8,128)(2,1)S(1)} %copy-done), kind=kOutput, calls=%fused_computation.1 | convolution fusion | flops 4294967296 | bytes 14680064 | tf_op jit(solution)/shard_map/dot_general | solution.py:29
  220.9 0.0 reduce-scatter.5.cloned.1.call-update
  220.9 93.4 %reduce-scatter.5.cloned.1.call-done = f32[2048,128]{0,1:T(8,128)} async-done(((f32[2048,1024]{0,1:T(8,128)}), f32[2048,128]{0,1:T(8,128)}) %reduce-scatter.5.cloned.1.call-update) | async-done | bytes 1048592 | tf_op jit(solution)/shard_map/reduce_scatter | solution.py:32
  314.3 2.5 copy.14
Async XLA Ops:
  7.2 144.0 %reduce-scatter.7.cloned.1.call-start = ((), (), s32[]{:S(2)}) async-start(), calls=%async_computation.4 | async-start | bytes 4325376 | tf_op jit(solution)/shard_map/reduce_scatter | solution.py:22
  23.7 290.6 %reduce-scatter.5.cloned.1.call-start = ((), (), s32[]{:S(2)}) async-start(), calls=%async_computation.3 | async-start | bytes 9437184 | tf_op jit(solution)/shard_map/reduce_scatter | solution.py:32
  151.1 62.9 %copy-start = (bf16[1024,2048]{1,0:T(8,128)(2,1)S(1)}, bf16[1024,2048]{1,0:T(8,128)(2,1)}, u32[]{:S(2)}) copy-start(bf16[1024,2048]{1,0:T(8,128)(2,1)} %param.3) | copy-start | bytes 12582916
Sparse Core Ops, SparseCore 0:
  23.8 127.3 reduce-scatter.6
  221.0 93.1 reduce-scatter.4
